TPU v7x, 256 devices: a whole 4x4x8 slice. The times are simulated.
256 devices in a mesh: dp: 8 (over y, core), seq: 32 (over z, x).
Axes of the slice: x: 4, y: 4, z: 8, core: 2. Of those that a mesh axis runs over, the one named last changes fastest.
Arguments:
- features: bfloat16 [8, 24576, 512], P('dp', 'seq'), may hold values from -12 to 12, as said below
- slot_kind: int32 [8, 96], P('dp', 'seq'), may hold values from 0 to 2, as said below
- block_gain: float32 [512], replicated, may hold values from 0.1 to 1.9
- block_shift: float32 [512], replicated, may hold values from -2 to 2
- block_weight: bfloat16 [4608, 512], replicated, may hold values from -0.09375 to 0.09375
- block_bias: float32 [512], replicated, may hold values from -2 to 2
- final_gain: float32 [512], replicated, may hold values from 0.1 to 1.9
- final_shift: float32 [512], replicated, may hold values from -2 to 2
- latent_weight: bfloat16 [512, 144], replicated, may hold values from -0.09375 to 0.09375
- latent_bias: float32 [16], replicated, may hold values from -2 to 2
- embed_weight: bfloat16 [64, 1152], P(None, 'dp'), may hold values from -0.75 to 0.75
- embed_bias: bfloat16 [1152], P('dp'), may hold values from -2 to 2
Outputs:
- sequence: bfloat16 [8, 4096, 1152], P('dp', 'seq')
Inputs may be any that keep to these rules, and one draw needn't show every extreme that they name: `slot_kind`: the live slots of a device (kind 1 or 2) come before its empty ones. In every dp group, the live slots of the devices with seq index below d number between 2 d and 2 d + 2, and 2 * 32 over the whole group; in every group some device has 3 live slots. `features`: finite values.
All inputs are finite; a program needn't handle non-finite values.
Results may differ from a plain program's by a relative error of at most 0.014.
Values may be sent and summed in bfloat16 or wider, within the bound.
A program may use at most 64 MiB of HBM per device.

v0:
```python
import jax
import jax.numpy as jnp
from jax import lax
from jax.sharding import PartitionSpec as P

GROUPS = 32
SLOT_ROWS = 32
SLOT_COLS = 8
LATENT_SHIFT = 0.0609
LATENT_SCALE = 1.5305
NORM_EPSILON = 1e-06
OFFSETS = [(-1, -1), (-1, 0), (-1, 1), (0, -1), (0, 0), (0, 1), (1, -1), (1, 0), (1, 1)]


def shifted(value, axis, steps):
    count = lax.axis_size(axis)
    leading, last = (max(0, -steps), min(count, count - steps))
    return lax.ppermute(value, axis, [(source, source + steps) for source in range(leading, last)])


def group_norm(values, slot_types, norm_gain, norm_shift):
    slot_count, height, across, channels = values.shape
    grouped = values.reshape(slot_count, 2, height // 2, across, GROUPS, channels // GROUPS)
    joined = (slot_types == 2)[:, None, None, None, None, None]
    half_centre = jnp.mean(grouped, axis=(2, 3, 5), keepdims=True)
    centre = jnp.where(joined, jnp.mean(half_centre, axis=1, keepdims=True), half_centre)
    centred = grouped - centre
    half_spread = jnp.mean(centred * centred, axis=(2, 3, 5), keepdims=True)
    spread = jnp.where(joined, jnp.mean(half_spread, axis=1, keepdims=True), half_spread)
    normed = (centred * lax.rsqrt(spread + NORM_EPSILON)).reshape(values.shape)
    return normed * norm_gain + norm_shift


def boundary_mask(slot_types, height, row_step, out_type):
    row_index = jnp.arange(height)
    edge_row = height // 2 if row_step < 0 else height // 2 - 1
    crossing = (slot_types == 1)[:, None] & (row_index == edge_row)[None, :]
    return jnp.where(crossing, 0.0, 1.0).astype(out_type)[:, :, None, None]


def neighbour(padded, slot_types, row_step, col_step):
    height = padded.shape[1] - 2
    across = padded.shape[2] - 2
    window = padded[
        :, 1 + row_step : 1 + row_step + height, 1 + col_step : 1 + col_step + across, :
    ]
    if row_step != 0:
        window = window * boundary_mask(slot_types, height, row_step, window.dtype)
    return window


def encode(
    slots,
    slot_types,
    block_gain,
    block_shift,
    block_weight,
    block_bias,
    final_gain,
    final_shift,
    latent_weight,
    latent_bias,
):
    slot_count, height, across, channels = slots.shape
    lat_width = latent_weight.shape[1] // 9
    first_act = jax.nn.silu(
        group_norm(slots.astype(jnp.float32), slot_types, block_gain, block_shift)
    ).astype(jnp.bfloat16)
    padded = jnp.pad(first_act, ((0, 0), (1, 1), (1, 1), (0, 0)))
    columns = jnp.concatenate(
        [neighbour(padded, slot_types, row_step, col_step) for row_step, col_step in OFFSETS],
        axis=-1,
    )
    conv_out = (
        jnp.dot(columns.reshape(-1, 9 * channels), block_weight, preferred_element_type=jnp.float32)
        + block_bias
    )
    inner = (
        (slots.reshape(-1, channels).astype(jnp.float32) + conv_out)
        .astype(jnp.bfloat16)
        .reshape(slots.shape)
    )
    second_act = jax.nn.silu(
        group_norm(inner.astype(jnp.float32), slot_types, final_gain, final_shift)
    ).astype(jnp.bfloat16)
    tap_terms = jnp.dot(
        second_act.reshape(-1, channels), latent_weight, preferred_element_type=jnp.float32
    )
    tap_terms = tap_terms.reshape(slot_count, height, across, 9 * lat_width)
    padded_terms = jnp.pad(tap_terms, ((0, 0), (1, 1), (1, 1), (0, 0)))
    latent = jnp.zeros((slot_count, height, across, lat_width), jnp.float32) + latent_bias
    for tap_number, (row_step, col_step) in enumerate(OFFSETS):
        piece_terms = padded_terms[..., tap_number * lat_width : (tap_number + 1) * lat_width]
        latent = latent + neighbour(piece_terms, slot_types, row_step, col_step)
    scaled = (latent - LATENT_SHIFT) * LATENT_SCALE
    patches = scaled.reshape(slot_count, height // 2, 2, across // 2, 2, lat_width).transpose(
        0, 1, 3, 2, 4, 5
    )
    return patches.reshape(slot_count * (height // 2) * (across // 2), 4 * lat_width).astype(
        jnp.bfloat16
    )


def local(
    features,
    slot_kind,
    block_gain,
    block_shift,
    block_weight,
    block_bias,
    final_gain,
    final_shift,
    latent_weight,
    latent_bias,
    embed_weight,
    embed_bias,
):
    seq_devices = lax.axis_size("seq")
    position = lax.axis_index("seq")
    slot_total = slot_kind.shape[1]
    channels = features.shape[2]
    all_types = lax.all_gather(slot_kind[0], "seq", axis=0, tiled=True)
    live_slots = (all_types.reshape(seq_devices, slot_total) > 0).astype(jnp.int32)
    counts = jnp.sum(live_slots, axis=1)
    starts = jnp.cumsum(counts) - counts
    embed_full, bias_full = (
        lax.all_gather(embed_weight, "dp", axis=1, tiled=True),
        lax.all_gather(embed_bias, "dp", axis=0, tiled=True),
    )
    own_slots = features[0].reshape(slot_total, SLOT_ROWS, SLOT_COLS, channels)
    carry_in = starts[position] - 2 * position
    slot_number = jnp.arange(2, dtype=jnp.int32)
    hid_width = embed_full.shape[1]
    patches = encode(
        own_slots,
        slot_kind[0],
        block_gain,
        block_shift,
        block_weight,
        block_bias,
        final_gain,
        final_shift,
        latent_weight,
        latent_bias,
    )
    tokens = (
        (
            jnp.dot(patches, embed_full, preferred_element_type=jnp.float32)
            + bias_full.astype(jnp.float32)
        )
        .astype(jnp.bfloat16)
        .reshape(slot_total, -1, hid_width)
    )
    padded = jnp.concatenate([tokens, jnp.zeros_like(tokens[:1])], axis=0)
    arrived = shifted(lax.dynamic_slice_in_dim(padded, 2 - carry_in, 2, 0), "seq", 1)
    kept = jnp.take(tokens, jnp.maximum(slot_number - carry_in, 0), axis=0)
    incoming = (slot_number < carry_in).reshape((2,) + (1,) * (tokens.ndim - 1))
    result = jnp.where(incoming, arrived, kept)
    return result.reshape(1, -1, hid_width)


def solution(mesh):
    in_specs = (
        P("dp", "seq", None),
        P("dp", "seq"),
        P(),
        P(),
        P(),
        P(),
        P(),
        P(),
        P(),
        P(),
        P(None, "dp"),
        P("dp"),
    )
    out_specs = P("dp", "seq", None)
    return jax.shard_map(local, mesh=mesh, in_specs=in_specs, out_specs=out_specs, check_vma=False)
```

profile of v0, /device:TPU:32, one launch (start us, length us, event | category | flops | bytes accessed | tf_op | source)
XLA Modules:
  0.0 126.7 jit_solution(9587615518974002790)
XLA Ops:
  0.0 8.2 %reshape.311 = f32[3,2,16,8,32,16]{5,4,3,2,1,0:T(8,128)} reshape(bf16[1,768,512]{2,1,0:T(8,128)(2,1)} %param.12) | data formatting | bytes 2359296 | tf_op jit(solution)/shard_map/convert_element_type | solution.py:67
  8.2 0.2 convert_element_type.117
  8.4 0.4 copy-done.12
  8.9 5.9 %reduce_sum.82 = f32[3,2,32]{2,1,0:T(2,128)S(1)} reduce(f32[3,2,16,8,32,16]{5,4,3,2,1,0:T(8,128)} %reshape.311, f32[]{:T(128)} %constant.57.clone.1), dimensions={2,3,5}, to_apply=%region_2.3 | reduce | flops 393024 | bytes 1573636 | tf_op jit(solution)/shard_map/reduce_sum | solution.py:25
  14.8 6.4 %multiply_reduce_fusion.1 = f32[3,2,32]{2,1,0:T(2,128)S(1)} fusion(f32[3,2,16,8,32,16]{5,4,3,2,1,0:T(8,128)} %reshape.311, f32[3,2,32]{2,1,0:T(2,128)S(1)} %broadcast_select_fusion.1), kind=kLoop, calls=%fused_computation.2 | loop fusion | flops 1179456 | bytes 1574400 | tf_op jit(solution)/shard_map/reduce_sum | solution.py:28
  21.4 0.3 mul.155
  21.6 1.1 mul.156
  22.7 0.2 sub.71
  23.0 1.7 %sub.72 = f32[3,32,512]{2,1,0:T(8,128)} reshape(f32[3,2,16,32,16]{4,3,2,1,0:T(8,128)S(1)} %sub.71) | data formatting | bytes 393216 | tf_op jit(solution)/shard_map/sub | solution.py:27
  24.8 1.6 %multiply_convert_fusion.1 = bf16[3,32,8,512]{3,2,1,0:T(8,128)(2,1)S(1)} fusion(f32[3,32,8,512]{3,2,1,0:T(8,128)S(1)} %bitcast.64, f32[512]{0:T(512)S(1)} %copy-done.5, f32[512]{0:T(512)S(1)} %copy-done.6, f32[3,32,512]{2,1,0:T(8,128)S(1)} %mul.156, f32[3,32,512]{2,1,0:T(8,128)} %sub.72), kind=kLoop, calls=%fused_computation.28 | loop fusion | flops 3538944 | bytes 2756608 | tf_op jit(solution)/shard_map/convert_element_type | solution.py:68
  26.4 0.3 fusion.6
  26.6 0.2 fusion.8
  26.9 0.3 fusion.10
  27.2 0.2 fusion.11
  27.4 0.5 copy-done.3
  27.8 0.5 constant_dynamic-update-slice_fusion
  28.3 0.2 fusion.12
  28.5 0.3 fusion.14
  28.8 0.2 fusion.16
  29.1 0.3 fusion.18
  29.3 0.6 copy-done.2
  29.9 3.8 %fusion.4 = f32[768,512]{1,0:T(8,128)S(1)} fusion(bf16[768,4608]{1,0:T(8,128)(2,1)S(1)} %bitcast.71, bf16[4608,512]{1,0:T(8,128)(2,1)S(1)} %bitcast.75, f32[512]{0:T(512)S(1)} %copy-done.10, bf16[1,768,512]{2,1,0:T(8,128)(2,1)S(1)} %copy-done.2), kind=kOutput, calls=%fused_computation.29 | convolution fusion | flops 3625844736 | bytes 14157824 | tf_op jit(solution)/shard_map/dot_general | solution.py:75
  33.7 6.9 %reshape.312 = f32[3,2,16,8,32,16]{5,4,3,2,1,0:T(8,128)} reshape(f32[768,512]{1,0:T(8,128)S(1)} %fusion.4) | data formatting | bytes 3145728 | tf_op jit(solution)/shard_map/convert_element_type | solution.py:84
  40.6 5.9 %reduce_sum.86 = f32[3,2,32]{2,1,0:T(2,128)S(1)} reduce(f32[3,2,16,8,32,16]{5,4,3,2,1,0:T(8,128)} %reshape.312, f32[]{:T(128)} %constant.57.clone.1), dimensions={2,3,5}, to_apply=%region_6.7 | reduce | flops 393024 | bytes 1573636 | tf_op jit(solution)/shard_map/reduce_sum | solution.py:25
  46.6 6.4 %multiply_reduce_fusion = f32[3,2,32]{2,1,0:T(2,128)S(1)} fusion(f32[3,2,16,8,32,16]{5,4,3,2,1,0:T(8,128)} %reshape.312, f32[3,2,32]{2,1,0:T(2,128)S(1)} %broadcast_select_fusion), kind=kLoop, calls=%fused_computation.1 | loop fusion | flops 1179456 | bytes 1574400 | tf_op jit(solution)/shard_map/reduce_sum | solution.py:28
  53.1 0.3 mul.171
  53.4 1.1 mul.172
  54.5 0.2 sub.77
  54.7 1.7 %sub.78 = f32[3,32,512]{2,1,0:T(8,128)} reshape(f32[3,2,16,32,16]{4,3,2,1,0:T(8,128)S(1)} %sub.77) | data formatting | bytes 393216 | tf_op jit(solution)/shard_map/sub | solution.py:27
  56.5 1.4 %multiply_convert_fusion = bf16[768,512]{1,0:T(8,128)(2,1)S(1)} fusion(f32[768,512]{1,0:T(8,128)S(1)} %fusion.4, f32[512]{0:T(512)S(1)} %copy-done.7, f32[512]{0:T(512)S(1)} %copy-done.8, f32[3,32,512]{2,1,0:T(8,128)S(1)} %mul.172, f32[3,32,512]{2,1,0:T(8,128)} %sub.78), kind=kLoop, calls=%fused_computation.27 | loop fusion | flops 3538944 | bytes 2756608 | tf_op jit(solution)/shard_map/convert_element_type | solution.py:85
  58.0 0.4 fusion.37
  58.4 1.0 fusion.36
  59.3 0.1 copy.22
  59.5 0.1 convert_element_type.113
  59.6 0.6 dynamic-slice.1
  60.9 0.2 dynamic-update-slice.1
  61.2 14.9 %all-reduce.4 = bf16[1152]{0:T(1024)(128)(2,1)S(1)} all-reduce(bf16[1152]{0:T(1024)(128)(2,1)S(1)} %dynamic-update-slice.1), channel_id=1, replica_groups=mesh['dp'=8,'seq'=32] {'dp'}, use_global_device_ids=true, to_apply=%add.4 | all-reduce | flops 1152 | bytes 4608
  76.0 12.8 %all-gather.1 = bf16[8,144,64]{1,2,0:T(8,128)(2,1)S(1)} all-gather(bf16[1,144,64]{1,2,0:T(8,128)(2,1)S(1)} %bitcast.72), channel_id=1, replica_groups=mesh['dp'=8,'seq'=32] {'dp'}, dimensions={0}, use_global_device_ids=true | all-gather | bytes 165888 | tf_op jit(solution)/shard_map/all_gather | solution.py:127
  88.9 0.1 copy.19
  89.0 0.3 reshape.337
  89.3 0.6 dynamic-slice
  90.6 22.4 %all-reduce.3 = s32[96]{0:T(128)S(1)} all-reduce(s32[96]{0:T(128)S(1)} %bitcast_dynamic-update-slice_fusion), channel_id=2, replica_groups=mesh['dp'=8,'seq'=32] {'seq'}, use_global_device_ids=true, to_apply=%add.3 | all-reduce | flops 96 | bytes 768
  113.6 0.6 dynamic_slice.6
  114.8 0.3 fusion
  115.2 2.5 %collective-permute-start = (bf16[2,64,1152]{2,1,0:T(8,128)(2,1)S(1)}, bf16[2,64,1152]{2,1,0:T(8,128)(2,1)S(1)}, u32[]{:S(2)}, u32[]{:S(2)}) collective-permute-start(bf16[2,64,1152]{2,1,0:T(8,128)(2,1)S(1)} %pad_dynamic-slice_fusion), channel_id=1, source_target_pairs={{0,1},{1,2},{2,3},{3,4},{4,5},{5,6},{6,7},{7,8},{8,9},{9,10},{10,1... | collective-permute-start | bytes 884744 | tf_op jit(solution)/shard_map/ppermute | solution.py:18
  117.7 0.6 gather_fusion
  118.3 7.6 %collective-permute-done = bf16[2,64,1152]{2,1,0:T(8,128)(2,1)S(1)} collective-permute-done((bf16[2,64,1152]{2,1,0:T(8,128)(2,1)S(1)}, bf16[2,64,1152]{2,1,0:T(8,128)(2,1)S(1)}, u32[]{:S(2)}, u32[]{:S(2)}) %collective-permute-start) | collective-permute-done | bytes 294944 | tf_op jit(solution)/shard_map/ppermute | solution.py:18
  125.9 0.8 select_select_fusion
  (62 shorter events, 1.2 us)
Async XLA Ops:
  0.0 57.9 %copy-start = (bf16[512,144]{0,1:T(8,128)(2,1)S(1)}, bf16[512,144]{0,1:T(8,128)(2,1)}, u32[]{:S(2)}) copy-start(bf16[512,144]{0,1:T(8,128)(2,1)} %param.20) | copy-start | bytes 442372
  0.0 8.2 %copy-start.1 = (bf16[1,768,512]{2,1,0:T(8,128)(2,1)S(1)}, bf16[1,768,512]{2,1,0:T(8,128)(2,1)}, u32[]{:S(2)}) copy-start(bf16[1,768,512]{2,1,0:T(8,128)(2,1)} %param.12) | copy-start | bytes 2359300
  8.2 0.7 copy-start.12
  22.7 2.1 %copy-start.5 = (f32[512]{0:T(512)S(1)}, f32[512]{0:T(512)}, u32[]{:S(2)}) copy-start(f32[512]{0:T(512)} %param.15) | copy-start | bytes 6148
  22.7 2.1 %copy-start.6 = (f32[512]{0:T(512)S(1)}, f32[512]{0:T(512)}, u32[]{:S(2)}) copy-start(f32[512]{0:T(512)} %param.14) | copy-start | bytes 6148
  24.8 4.5 %slice-start = ((s8[4718592]{0:T(1024)(128)(4,1)}), s8[4194304]{0:T(1024)(128)(4,1)S(1)}, s32[]{:S(2)}) async-start(s8[4718592]{0:T(1024)(128)(4,1)} %bitcast.74), calls=%async_computation | async-start | bytes 8388608
  26.9 0.9 copy-start.3
  27.8 1.5 %slice-start.1 = ((s8[4718592]{0:T(1024)(128)(4,1)}), s8[524288]{0:T(1024)(128)(4,1)S(1)}, s32[]{:S(2)}) async-start(s8[4718592]{0:T(1024)(128)(4,1)} %bitcast.74), calls=%async_computation.1 | async-start | bytes 1048576
  28.8 1.1 copy-start.2
  28.8 1.1 copy-start.10
  54.4 2.0 %copy-start.7 = (f32[512]{0:T(512)S(1)}, f32[512]{0:T(512)}, u32[]{:S(2)}) copy-start(f32[512]{0:T(512)} %param.19) | copy-start | bytes 6148
  54.4 2.0 %copy-start.8 = (f32[512]{0:T(512)S(1)}, f32[512]{0:T(512)}, u32[]{:S(2)}) copy-start(f32[512]{0:T(512)} %param.18) | copy-start | bytes 6148
  56.5 1.9 %copy-start.9 = (f32[16]{0:T(128)S(1)}, f32[16]{0:T(128)}, u32[]{:S(2)}) copy-start(f32[16]{0:T(128)} %param.21) | copy-start | bytes 196
  57.9 1.7 %copy-start.14 = (u32[256]{0:T(256)S(1)}, u32[256]{0:T(256)}, u32[]{:S(2)}) copy-start(u32[256]{0:T(256)} %constant.85) | copy-start | bytes 3076
  57.9 3.0 %copy-start.11 = (bf16[144]{0:T(256)(128)(2,1)S(1)}, bf16[144]{0:T(256)(128)(2,1)}, u32[]{:S(2)}) copy-start(bf16[144]{0:T(256)(128)(2,1)} %param.23) | copy-start | bytes 868
  57.9 18.1 %copy-start.4 = (bf16[64,144]{1,0:T(8,128)(2,1)S(1)}, bf16[64,144]{1,0:T(8,128)(2,1)}, u32[]{:S(2)}) copy-start(bf16[64,144]{1,0:T(8,128)(2,1)} %param.22) | copy-start | bytes 55300
  58.3 30.9 %copy-start.13 = (u32[256]{0:T(256)S(1)}, u32[256]{0:T(256)}, u32[]{:S(2)}) copy-start(u32[256]{0:T(256)} %constant.80) | copy-start | bytes 3076
  115.2 10.7 %collective-permute-start = (bf16[2,64,1152]{2,1,0:T(8,128)(2,1)S(1)}, bf16[2,64,1152]{2,1,0:T(8,128)(2,1)S(1)}, u32[]{:S(2)}, u32[]{:S(2)}) collective-permute-start(bf16[2,64,1152]{2,1,0:T(8,128)(2,1)S(1)} %pad_dynamic-slice_fusion), channel_id=1, source_target_pairs={{0,1},{1,2},{2,3},{3,4},{4,5},{5,6},{6,7},{7,8},{8,9},{9,10},{10,1... | collective-permute-start | bytes 884744 | tf_op jit(solution)/shard_map/ppermute | solution.py:18
where the time goes:
time: 127 us
  blocking collectives  50.1 us (39%)
  other arithmetic  32.4 us (26%)
  local copies, waits for them, and re-layouts  27.3 us (21%)
  waiting for transfers between devices  7.57 us (6%)
  matrix products  4.42 us (3%)
  starting transfers between devices  2.51 us (2%)
  between operations  2.4 us (2%)
    unnamed x2, blocking collectives  37.3 us
    all_gather x1, blocking collectives, local(): lax.all_gather(embed_weight, 'dp', axis=1, tiled=True)  12.8 us
    reduce_sum x2, other arithmetic, group_norm(): half_spread = jnp.mean(centred * centred, axis=(2, 3, 5), keepdims=True)  12.8 us
    reduce_sum x2, other arithmetic, group_norm(): half_centre = jnp.mean(grouped, axis=(2, 3, 5), keepdims=True)  11.7 us
    convert_element_type x1, local copies, waits for them, and re-layouts, encode(): slots.astype(jnp.float32)  8.2 us
    ppermute x1, waiting for transfers between devices, shifted(): lax.ppermute(value, axis, [(source, source + steps) for source in range(l...  7.57 us
    convert_element_type x1, local copies, waits for them, and re-layouts, encode(): inner.astype(jnp.float32)  6.89 us
    sub x4, local copies, waits for them, and re-layouts, group_norm(): centred = grouped - centre  3.99 us
  transfers between devices with their start and end apart: 1, of which 1 were waited for; matrix products, arithmetic and copies ran while one was open for 0% of the time, Pallas kernels for 0%

commit v1 on v0

--- a/solution.py
+++ b/solution.py
@@ -124,7 +124,9 @@
     counts = jnp.sum(live_slots, axis=1)
     starts = jnp.cumsum(counts) - counts
     embed_full, bias_full = (
-        lax.all_gather(embed_weight, "dp", axis=1, tiled=True),
+        jnp.concatenate(
+            lax.all_to_all(jnp.stack([embed_weight] * lax.axis_size("dp")), "dp", 0, 0), axis=1
+        ),
         lax.all_gather(embed_bias, "dp", axis=0, tiled=True),
     )
     own_slots = features[0].reshape(slot_total, SLOT_ROWS, SLOT_COLS, channels)

time: 127 us -> 122 us (0.961)
  blocking collectives: 50.1 us -> 37.8 us
  starting transfers between devices: 2.51 us -> 6.98 us
  local copies, waits for them, and re-layouts: 27.3 us -> 30 us
    all_gather x1 -> x0, blocking collectives: 12.8 us -> none  [local(): lax.all_gather(embed_weight, 'dp', axis=1, tiled=True)]
    all_to_all x0 -> x1, starting transfers between devices: none -> 4.47 us  [local(): lax.all_to_all(jnp.stack([embed_weight] * lax.axis_size('dp')), 'dp', 0, 0)]
    another operation x1 -> x2, local copies, waits for them, and re-layouts: 0.09 us -> 1.6 us  [the longest x1 1.51 us: local(): jnp.stack([embed_weight] * lax.axis_size('dp'))]
    reshape x0 -> x2, local copies, waits for them, and re-layouts: none -> 1.36 us  [local(): jnp.concatenate(lax.all_to_all(jnp.stack([embed_weight] * lax.axis_size('...]
    unnamed x43 -> x40, local copies, waits for them, and re-layouts: 3.69 us -> 3.59 us
  transfers between devices with their start and end apart: 1 -> 2, of which waited for: 1 -> 1; matrix products, arithmetic and copies ran while one was open for 0% -> 50% of each run, Pallas kernels for 0% -> 0%
where the time goes in v1:
time: 122 us
  blocking collectives  37.8 us (31%)
  other arithmetic  32.4 us (27%)
  local copies, waits for them, and re-layouts  30 us (25%)
  waiting for transfers between devices  7.57 us (6%)
  starting transfers between devices  6.98 us (6%)
  matrix products  4.43 us (4%)
  between operations  2.52 us (2%)
    unnamed x2, blocking collectives  37.8 us
    reduce_sum x2, other arithmetic, group_norm(): half_spread = jnp.mean(centred * centred, axis=(2, 3, 5), keepdims=True)  12.8 us
    reduce_sum x2, other arithmetic, group_norm(): half_centre = jnp.mean(grouped, axis=(2, 3, 5), keepdims=True)  11.7 us
    convert_element_type x1, local copies, waits for them, and re-layouts, encode(): slots.astype(jnp.float32)  8.2 us
    ppermute x1, waiting for transfers between devices, shifted(): lax.ppermute(value, axis, [(source, source + steps) for source in range(l...  7.57 us
    convert_element_type x1, local copies, waits for them, and re-layouts, encode(): inner.astype(jnp.float32)  6.89 us
    all_to_all x1, starting transfers between devices, local(): lax.all_to_all(jnp.stack([embed_weight] * lax.axis_size('dp')), 'dp', 0, 0)  4.47 us
    sub x4, local copies, waits for them, and re-layouts, group_norm(): centred = grouped - centre  3.98 us
  transfers between devices with their start and end apart: 2, of which 1 were waited for; matrix products, arithmetic and copies ran while one was open for 50% of the time, Pallas kernels for 0%

profile of v1, /device:TPU:32, one launch (start us, length us, event | category | flops | bytes accessed | tf_op | source)
XLA Modules:
  0.0 121.6 jit_solution(14549827671538975500)
XLA Ops:
  0.0 1.5 %stack.2 = bf16[8,64,144]{2,1,0:T(8,128)(2,1)} broadcast(bf16[64,144]{1,0:T(8,128)(2,1)} %param.22), dimensions={1,2} | broadcast | bytes 165888 | tf_op jit(solution)/shard_map/stack | solution.py:128
  1.5 4.5 %all-to-all-start = ((bf16[8,64,144]{2,1,0:T(8,128)(2,1)}), bf16[8,64,144]{2,1,0:T(8,128)(2,1)}, u32[]{:S(2)}, u32[]{:S(2)}) async-start(bf16[8,64,144]{2,1,0:T(8,128)(2,1)} %stack.2), calls=%async_computation | async-start | bytes 524288 | tf_op jit(solution)/shard_map/all_to_all | solution.py:128
  6.0 8.2 %reshape.321 = f32[3,2,16,8,32,16]{5,4,3,2,1,0:T(8,128)} reshape(bf16[1,768,512]{2,1,0:T(8,128)(2,1)} %param.12) | data formatting | bytes 2359296 | tf_op jit(solution)/shard_map/convert_element_type | solution.py:67
  14.2 0.2 convert_element_type.117
  14.4 0.4 copy-done.11
  14.9 5.9 %reduce_sum.82 = f32[3,2,32]{2,1,0:T(2,128)S(1)} reduce(f32[3,2,16,8,32,16]{5,4,3,2,1,0:T(8,128)} %reshape.321, f32[]{:T(128)} %constant.57.clone.1), dimensions={2,3,5}, to_apply=%region_2.3 | reduce | flops 393024 | bytes 1573636 | tf_op jit(solution)/shard_map/reduce_sum | solution.py:25
  20.8 6.4 %multiply_reduce_fusion.1 = f32[3,2,32]{2,1,0:T(2,128)S(1)} fusion(f32[3,2,16,8,32,16]{5,4,3,2,1,0:T(8,128)} %reshape.321, f32[3,2,32]{2,1,0:T(2,128)S(1)} %broadcast_select_fusion.1), kind=kLoop, calls=%fused_computation.2 | loop fusion | flops 1179456 | bytes 1574400 | tf_op jit(solution)/shard_map/reduce_sum | solution.py:28
  27.3 0.3 mul.155
  27.6 1.1 mul.156
  28.7 0.2 sub.71
  28.9 1.7 %sub.72 = f32[3,32,512]{2,1,0:T(8,128)} reshape(f32[3,2,16,32,16]{4,3,2,1,0:T(8,128)S(1)} %sub.71) | data formatting | bytes 393216 | tf_op jit(solution)/shard_map/sub | solution.py:27
  30.8 1.6 %multiply_convert_fusion.1 = bf16[3,32,8,512]{3,2,1,0:T(8,128)(2,1)S(1)} fusion(f32[3,32,8,512]{3,2,1,0:T(8,128)S(1)} %bitcast.60, f32[512]{0:T(512)S(1)} %copy-done.4, f32[512]{0:T(512)S(1)} %copy-done.5, f32[3,32,512]{2,1,0:T(8,128)S(1)} %mul.156, f32[3,32,512]{2,1,0:T(8,128)} %sub.72), kind=kLoop, calls=%fused_computation.28 | loop fusion | flops 3538944 | bytes 2756608 | tf_op jit(solution)/shard_map/convert_element_type | solution.py:68
  32.4 0.3 fusion.6
  32.6 0.2 fusion.8
  32.9 0.3 fusion.10
  33.1 0.2 fusion.11
  33.3 0.5 copy-done.3
  33.8 0.5 constant_dynamic-update-slice_fusion
  34.3 0.2 fusion.12
  34.5 0.3 fusion.14
  34.8 0.2 fusion.16
  35.0 0.3 fusion.18
  35.3 0.6 copy-done.2
  35.9 3.8 %fusion.4 = f32[768,512]{1,0:T(8,128)S(1)} fusion(bf16[768,4608]{1,0:T(8,128)(2,1)S(1)} %bitcast.67, bf16[4608,512]{1,0:T(8,128)(2,1)S(1)} %bitcast.70, f32[512]{0:T(512)S(1)} %copy-done.9, bf16[1,768,512]{2,1,0:T(8,128)(2,1)S(1)} %copy-done.2), kind=kOutput, calls=%fused_computation.29 | convolution fusion | flops 3625844736 | bytes 14157824 | tf_op jit(solution)/shard_map/dot_general | solution.py:75
  39.7 6.9 %reshape.322 = f32[3,2,16,8,32,16]{5,4,3,2,1,0:T(8,128)} reshape(f32[768,512]{1,0:T(8,128)S(1)} %fusion.4) | data formatting | bytes 3145728 | tf_op jit(solution)/shard_map/convert_element_type | solution.py:84
  46.6 5.9 %reduce_sum.86 = f32[3,2,32]{2,1,0:T(2,128)S(1)} reduce(f32[3,2,16,8,32,16]{5,4,3,2,1,0:T(8,128)} %reshape.322, f32[]{:T(128)} %constant.57.clone.1), dimensions={2,3,5}, to_apply=%region_6.7 | reduce | flops 393024 | bytes 1573636 | tf_op jit(solution)/shard_map/reduce_sum | solution.py:25
  52.6 6.4 %multiply_reduce_fusion = f32[3,2,32]{2,1,0:T(2,128)S(1)} fusion(f32[3,2,16,8,32,16]{5,4,3,2,1,0:T(8,128)} %reshape.322, f32[3,2,32]{2,1,0:T(2,128)S(1)} %broadcast_select_fusion), kind=kLoop, calls=%fused_computation.1 | loop fusion | flops 1179456 | bytes 1574400 | tf_op jit(solution)/shard_map/reduce_sum | solution.py:28
  59.1 0.3 mul.171
  59.4 1.1 mul.172
  60.4 0.2 sub.77
  60.7 1.7 %sub.78 = f32[3,32,512]{2,1,0:T(8,128)} reshape(f32[3,2,16,32,16]{4,3,2,1,0:T(8,128)S(1)} %sub.77) | data formatting | bytes 393216 | tf_op jit(solution)/shard_map/sub | solution.py:27
  62.4 1.4 %multiply_convert_fusion = bf16[768,512]{1,0:T(8,128)(2,1)S(1)} fusion(f32[768,512]{1,0:T(8,128)S(1)} %fusion.4, f32[512]{0:T(512)S(1)} %copy-done.6, f32[512]{0:T(512)S(1)} %copy-done.7, f32[3,32,512]{2,1,0:T(8,128)S(1)} %mul.172, f32[3,32,512]{2,1,0:T(8,128)} %sub.78), kind=kLoop, calls=%fused_computation.27 | loop fusion | flops 3538944 | bytes 2756608 | tf_op jit(solution)/shard_map/convert_element_type | solution.py:85
  63.9 0.4 fusion.37
  64.3 1.0 fusion.36
  65.4 0.1 convert_element_type.113
  65.6 0.7 dynamic-slice.1
  67.0 0.2 dynamic-update-slice.1
  67.2 15.4 %all-reduce.4 = bf16[1152]{0:T(1024)(128)(2,1)S(1)} all-reduce(bf16[1152]{0:T(1024)(128)(2,1)S(1)} %dynamic-update-slice.1), channel_id=1, replica_groups=mesh['dp'=8,'seq'=32] {'dp'}, use_global_device_ids=true, to_apply=%add.4 | all-reduce | flops 1152 | bytes 4608
  82.6 0.7 dynamic-slice
  84.1 22.4 %all-reduce.3 = s32[96]{0:T(128)S(1)} all-reduce(s32[96]{0:T(128)S(1)} %bitcast_dynamic-update-slice_fusion), channel_id=2, replica_groups=mesh['dp'=8,'seq'=32] {'seq'}, use_global_device_ids=true, to_apply=%add.3 | all-reduce | flops 96 | bytes 768
  107.0 0.7 dynamic_slice.6
  108.4 1.1 copy.18
  109.5 0.3 reshape.315
  109.8 0.3 fusion
  110.1 2.5 %collective-permute-start = (bf16[2,64,1152]{2,1,0:T(8,128)(2,1)S(1)}, bf16[2,64,1152]{2,1,0:T(8,128)(2,1)S(1)}, u32[]{:S(2)}, u32[]{:S(2)}) collective-permute-start(bf16[2,64,1152]{2,1,0:T(8,128)(2,1)S(1)} %pad_dynamic-slice_fusion), channel_id=1, source_target_pairs={{0,1},{1,2},{2,3},{3,4},{4,5},{5,6},{6,7},{7,8},{8,9},{9,10},{10,1... | collective-permute-start | bytes 884744 | tf_op jit(solution)/shard_map/ppermute | solution.py:18
  112.6 0.6 gather_fusion
  113.2 7.6 %collective-permute-done = bf16[2,64,1152]{2,1,0:T(8,128)(2,1)S(1)} collective-permute-done((bf16[2,64,1152]{2,1,0:T(8,128)(2,1)S(1)}, bf16[2,64,1152]{2,1,0:T(8,128)(2,1)S(1)}, u32[]{:S(2)}, u32[]{:S(2)}) %collective-permute-start) | collective-permute-done | bytes 294944 | tf_op jit(solution)/shard_map/ppermute | solution.py:18
  120.8 0.8 select_select_fusion
  (62 shorter events, 1.4 us)
Async XLA Ops:
  0.0 63.9 %copy-start = (bf16[512,144]{0,1:T(8,128)(2,1)S(1)}, bf16[512,144]{0,1:T(8,128)(2,1)}, u32[]{:S(2)}) copy-start(bf16[512,144]{0,1:T(8,128)(2,1)} %param.20) | copy-start | bytes 442372
  1.5 106.9 %all-to-all-start = ((bf16[8,64,144]{2,1,0:T(8,128)(2,1)}), bf16[8,64,144]{2,1,0:T(8,128)(2,1)}, u32[]{:S(2)}, u32[]{:S(2)}) async-start(bf16[8,64,144]{2,1,0:T(8,128)(2,1)} %stack.2), calls=%async_computation | async-start | bytes 524288 | tf_op jit(solution)/shard_map/all_to_all | solution.py:128
  6.0 8.2 %copy-start.1 = (bf16[1,768,512]{2,1,0:T(8,128)(2,1)S(1)}, bf16[1,768,512]{2,1,0:T(8,128)(2,1)}, u32[]{:S(2)}) copy-start(bf16[1,768,512]{2,1,0:T(8,128)(2,1)} %param.12) | copy-start | bytes 2359300
  14.2 0.7 copy-start.11
  28.7 2.1 %copy-start.4 = (f32[512]{0:T(512)S(1)}, f32[512]{0:T(512)}, u32[]{:S(2)}) copy-start(f32[512]{0:T(512)} %param.15) | copy-start | bytes 6148
  28.7 2.1 %copy-start.5 = (f32[512]{0:T(512)S(1)}, f32[512]{0:T(512)}, u32[]{:S(2)}) copy-start(f32[512]{0:T(512)} %param.14) | copy-start | bytes 6148
  30.8 4.5 %slice-start = ((s8[4718592]{0:T(1024)(128)(4,1)}), s8[4194304]{0:T(1024)(128)(4,1)S(1)}, s32[]{:S(2)}) async-start(s8[4718592]{0:T(1024)(128)(4,1)} %bitcast.69), calls=%async_computation.1 | async-start | bytes 8388608
  32.9 0.9 copy-start.3
  33.8 1.5 %slice-start.1 = ((s8[4718592]{0:T(1024)(128)(4,1)}), s8[524288]{0:T(1024)(128)(4,1)S(1)}, s32[]{:S(2)}) async-start(s8[4718592]{0:T(1024)(128)(4,1)} %bitcast.69), calls=%async_computation.2 | async-start | bytes 1048576
  34.8 1.1 copy-start.2
  34.8 1.1 copy-start.9
  60.4 2.0 %copy-start.6 = (f32[512]{0:T(512)S(1)}, f32[512]{0:T(512)}, u32[]{:S(2)}) copy-start(f32[512]{0:T(512)} %param.19) | copy-start | bytes 6148
  60.4 2.0 %copy-start.7 = (f32[512]{0:T(512)S(1)}, f32[512]{0:T(512)}, u32[]{:S(2)}) copy-start(f32[512]{0:T(512)} %param.18) | copy-start | bytes 6148
  62.4 1.9 %copy-start.8 = (f32[16]{0:T(128)S(1)}, f32[16]{0:T(128)}, u32[]{:S(2)}) copy-start(f32[16]{0:T(128)} %param.21) | copy-start | bytes 196
  63.9 1.7 %copy-start.13 = (u32[256]{0:T(256)S(1)}, u32[256]{0:T(256)}, u32[]{:S(2)}) copy-start(u32[256]{0:T(256)} %constant.85) | copy-start | bytes 3076
  63.9 3.1 %copy-start.10 = (bf16[144]{0:T(256)(128)(2,1)S(1)}, bf16[144]{0:T(256)(128)(2,1)}, u32[]{:S(2)}) copy-start(bf16[144]{0:T(256)(128)(2,1)} %param.23) | copy-start | bytes 868
  63.9 18.7 %copy-start.12 = (u32[256]{0:T(256)S(1)}, u32[256]{0:T(256)}, u32[]{:S(2)}) copy-start(u32[256]{0:T(256)} %constant.80) | copy-start | bytes 3076
  110.1 10.7 %collective-permute-start = (bf16[2,64,1152]{2,1,0:T(8,128)(2,1)S(1)}, bf16[2,64,1152]{2,1,0:T(8,128)(2,1)S(1)}, u32[]{:S(2)}, u32[]{:S(2)}) collective-permute-start(bf16[2,64,1152]{2,1,0:T(8,128)(2,1)S(1)} %pad_dynamic-slice_fusion), channel_id=1, source_target_pairs={{0,1},{1,2},{2,3},{3,4},{4,5},{5,6},{6,7},{7,8},{8,9},{9,10},{10,1... | collective-permute-start | bytes 884744 | tf_op jit(solution)/shard_map/ppermute | solution.py:18
